TPU v7x, 32 devices: a whole 2x2x4 slice. The times are simulated.
32 devices in a mesh: freq: 4 (over y, x), panel: 8 (over z, core).
Axes of the slice: x: 2, y: 2, z: 4, core: 2. Of those that a mesh axis runs over, the one named last changes fastest.
Arguments:
- fields: bfloat16 [128, 16, 16384], P('freq', None, 'panel'), may hold values from -6 to 6
- quad_index: int32 [16384], P('panel'), may hold values from 0 to 5
- band_width: int32 [128], P('freq'), may hold values from 1 to 64, as said below
Outputs:
- pair_blocks: float32 [128, 16384], P('freq', 'panel')
Inputs may be any that keep to these rules, and one draw needn't show every extreme that they name: `band_width`: some frequency has band width exactly 64.
All inputs are finite; a program needn't handle non-finite values.
Results may differ from a plain program's by a relative error of at most 0.0029.
Values may be sent and summed in bfloat16 or wider, within the bound.
A program may use at most 128 MiB of HBM per device.

v0:
```python
import math

import jax
import jax.numpy as jnp
from jax import lax
from jax.sharding import PartitionSpec as P

COMP = 16
REACH = 2


QUAD_TABLE = (0.2, 0.45, 0.8, 1.1, 1.6, 2.3)


def shifted(x, axis, by):
    devices = lax.axis_size(axis)
    pairs = [(i, i + by) for i in range(devices) if 0 <= i + by < devices]
    return lax.ppermute(x, axis, pairs)


def local(fields, quad_index, band_width):
    freq_local = fields.shape[0]
    panel_local = fields.shape[2]
    band = REACH * freq_local
    table = jnp.asarray(QUAD_TABLE, jnp.float32)
    matches = quad_index[None, :] == jnp.arange(6, dtype=jnp.int32)[:, None]
    weight = jnp.sum(jnp.where(matches, table[:, None], jnp.float32(0.0)), 0)
    scaled = (fields.astype(jnp.float32) * weight).astype(jnp.bfloat16)
    own_rows = scaled.reshape(freq_local * COMP, panel_local)
    partners = [fields]
    for distance in range(1, REACH + 1):
        partners.append(shifted(fields, "freq", -distance))
    grams = []
    for partner in partners:
        grams.append(
            lax.dot_general(
                own_rows,
                partner.reshape(freq_local * COMP, panel_local),
                (((1,), (1,)), ((), ())),
                preferred_element_type=jnp.float32,
            )
        )
    stacked = jnp.concatenate(grams, 1).reshape(freq_local, COMP, (REACH + 1) * freq_local, COMP)

    def pick_band(block, row_index):
        return lax.dynamic_slice_in_dim(block, row_index + 1, band, 1)

    picked = jax.vmap(pick_band)(stacked, jnp.arange(freq_local, dtype=jnp.int32))
    picked = picked.transpose(0, 2, 1, 3)
    offsets = jnp.arange(band, dtype=jnp.int32) + 1
    live_mask = offsets[None, :] <= band_width[:, None]
    picked = jnp.where(live_mask[:, :, None, None], picked, jnp.float32(0.0))
    panels_total = panel_local * lax.axis_size("panel")
    terms = picked.reshape(freq_local, band * COMP * COMP) * jnp.float32(
        1.0 / math.sqrt(panels_total)
    )
    return lax.psum_scatter(terms, "panel", scatter_dimension=1, tiled=True)


def solution(mesh):
    placed = (P("freq", None, "panel"), P("panel"), P("freq"))
    return jax.shard_map(
        local, mesh=mesh, in_specs=placed, out_specs=P("freq", "panel"), check_vma=False
    )
```

profile of v0, /device:TPU:26, one launch (start us, length us, event | category | flops | bytes accessed | tf_op | source)
XLA Modules:
  0.0 282.2 jit_solution(7882438305652038148)
XLA Ops:
  6.5 0.0 copy-start
  6.5 0.0 reduce-scatter.2.cloned.1.call-start
  6.5 2.6 collective-permute-start
  9.1 1.3 collective-permute-start.1
  10.4 0.8 select_reduce_fusion
  11.2 0.7 broadcast_compare_fusion
  12.0 2.0 multiply_convert_fusion
  14.0 0.0 copy-done
  14.0 1.3 fusion.4
  15.3 41.8 %collective-permute-done = bf16[32,16,2048]{2,1,0:T(8,128)(2,1)S(1)} collective-permute-done((bf16[32,16,2048]{2,1,0:T(8,128)(2,1)}, bf16[32,16,2048]{2,1,0:T(8,128)(2,1)S(1)}, u32[]{:S(2)}, u32[]{:S(2)}) %collective-permute-start) | collective-permute-done | bytes 2097184 | tf_op jit(solution)/shard_map/ppermute | solution.py:18
  57.1 1.3 fusion.5
  58.4 43.6 %collective-permute-done.1 = bf16[32,16,2048]{2,1,0:T(8,128)(2,1)S(1)} collective-permute-done((bf16[32,16,2048]{2,1,0:T(8,128)(2,1)}, bf16[32,16,2048]{2,1,0:T(8,128)(2,1)S(1)}, u32[]{:S(2)}, u32[]{:S(2)}) %collective-permute-start.1) | collective-permute-done | bytes 2097184 | tf_op jit(solution)/shard_map/ppermute | solution.py:18
  102.0 1.3 fusion.6
  103.3 0.3 pad_maximum_fusion
  103.6 13.1 %reshape.83 = f32[32,16,96,16]{1,0,3,2:T(8,128)} reshape(f32[512,1536]{0,1:T(8,128)S(1)} %pad_maximum_fusion) | data formatting | bytes 6291456 | tf_op jit(solution)/shard_map/reshape | solution.py:43
  116.7 26.6 %copy.11 = f32[32,16,96,16]{3,1,0,2:T(8,128)} copy(f32[32,16,96,16]{1,0,3,2:T(8,128)} %reshape.83) | data formatting | bytes 6291456 | tf_op jit(solution)/shard_map/reshape | solution.py:43
  143.3 16.8 %gather_fusion = f32[32,16,64,16]{3,1,2,0:T(8,128)} fusion(f32[32,16,96,16]{3,1,0,2:T(8,128)} %copy.11, s32[32]{0:T(128)S(1)} %fusion.3), kind=kCustom, calls=%fused_computation | custom fusion | bytes 4194816 | tf_op jit(solution)/shard_map/vmap()/gather | solution.py:46
  160.1 12.2 %multiply_bitcast_fusion = f32[32,64,16,16]{3,2,1,0:T(8,128)} fusion(f32[32,16,64,16]{3,1,2,0:T(8,128)} %gather_fusion, pred[32,64]{1,0:T(8,128)(4,1)S(1)} %broadcast_compare_fusion), kind=kLoop, calls=%fused_computation.1 | loop fusion | flops 1048576 | bytes 4196352 | tf_op jit(solution)/shard_map/mul | solution.py:54
  172.2 13.6 %copy.12 = f32[32,64,16,16]{0,3,2,1:T(8,128)} copy(f32[32,64,16,16]{3,2,1,0:T(8,128)} %multiply_bitcast_fusion) | data formatting | bytes 4194304 | tf_op jit(solution)/shard_map/mul | solution.py:54
  185.9 0.0 reduce-scatter.2.cloned.1.call-update
  185.9 87.2 %reduce-scatter.2.cloned.1.call-done = f32[32,2048]{0,1:T(8,128)} async-done(((f32[32,16384]{0,1:T(8,128)}), f32[32,2048]{0,1:T(8,128)}) %reduce-scatter.2.cloned.1.call-update) | async-done | bytes 262160 | tf_op jit(solution)/shard_map/reduce_scatter | solution.py:57
  273.2 2.2 copy.13
  (2 shorter events, 0.0 us)
Async XLA Ops:
  6.5 7.5 %copy-start = (bf16[32,16,2048]{2,1,0:T(8,128)(2,1)S(1)}, bf16[32,16,2048]{2,1,0:T(8,128)(2,1)}, u32[]{:S(2)}) copy-start(bf16[32,16,2048]{2,1,0:T(8,128)(2,1)} %param.4) | copy-start | bytes 6291460
  6.5 266.6 %reduce-scatter.2.cloned.1.call-start = ((), (), s32[]{:S(2)}) async-start(), calls=%async_computation.1 | async-start | bytes 9437184 | tf_op jit(solution)/shard_map/reduce_scatter | solution.py:57
  6.5 50.6 %collective-permute-start = (bf16[32,16,2048]{2,1,0:T(8,128)(2,1)}, bf16[32,16,2048]{2,1,0:T(8,128)(2,1)S(1)}, u32[]{:S(2)}, u32[]{:S(2)}) collective-permute-start(bf16[32,16,2048]{2,1,0:T(8,128)(2,1)} %param.4), channel_id=1, source_target_pairs={{8,0},{16,8},{24,16},{9,1},{17,9},{25,17},{10,2},{18,10},{26,18},{... | collective-permute-start | bytes 6291464 | tf_op jit(solution)/shard_map/ppermute | solution.py:18
  9.1 92.9 %collective-permute-start.1 = (bf16[32,16,2048]{2,1,0:T(8,128)(2,1)}, bf16[32,16,2048]{2,1,0:T(8,128)(2,1)S(1)}, u32[]{:S(2)}, u32[]{:S(2)}) collective-permute-start(bf16[32,16,2048]{2,1,0:T(8,128)(2,1)} %param.4), channel_id=1, source_target_pairs={{16,0},{24,8},{17,1},{25,9},{18,2},{26,10},{19,3},{27,11},{20,4},{... | collective-permute-start | bytes 6291464 | tf_op jit(solution)/shard_map/ppermute | solution.py:18
Sparse Core Ops, SparseCore 0:
  186.0 87.0 reduce-scatter.1
where the time goes:
time: 287 us; the launch traced here: 282 us
  waiting for transfers between devices  173 us (60%)
  local copies, waits for them, and re-layouts  72.4 us (25%)
  other arithmetic  16.1 us (6%)
  between operations  13.5 us (5%)
  starting transfers between devices  3.86 us (1%)
  matrix products  3.84 us (1%)
    reduce_scatter x1, waiting for transfers between devices, local(): return lax.psum_scatter(terms, 'panel', scatter_dimension=1, tiled=True)  87.2 us
    ppermute x2, waiting for transfers between devices, shifted(): return lax.ppermute(x, axis, pairs)  85.4 us
    reshape x2, local copies, waits for them, and re-layouts, local(): jnp.concatenate(grams, 1)  39.7 us
    gather x1, local copies, waits for them, and re-layouts, pick_band(): return lax.dynamic_slice_in_dim(block, row_index + 1, band, 1)  16.8 us
    mul x1, local copies, waits for them, and re-layouts, local(): picked.reshape(freq_local, band * COMP * COMP)  13.6 us
    mul x1, other arithmetic, local(): picked.reshape(freq_local, band * COMP * COMP)  12.2 us
  transfers between devices with their start and end apart: 3, of which 3 were waited for; matrix products, arithmetic and copies ran while one was open for 2% of the time, Pallas kernels for 0%

commit v1 on v0

--- a/solution.py
+++ b/solution.py
@@ -1,13 +1,18 @@
+import functools
 import math
 
 import jax
 import jax.numpy as jnp
 from jax import lax
+from jax.experimental import pallas as pl
+from jax.experimental.pallas import tpu as pltpu
 from jax.sharding import PartitionSpec as P
 
 COMP = 16
 REACH = 2
-
+LANES = 128
+CORES = 2
+MESH = pl.DeviceIdType.MESH
 
 QUAD_TABLE = (0.2, 0.45, 0.8, 1.1, 1.6, 2.3)
 
@@ -18,7 +23,7 @@
     return lax.ppermute(x, axis, pairs)
 
 
-def local(fields, quad_index, band_width):
+def plain(fields, quad_index, band_width):
     freq_local = fields.shape[0]
     panel_local = fields.shape[2]
     band = REACH * freq_local
@@ -57,8 +62,433 @@
     return lax.psum_scatter(terms, "panel", scatter_dimension=1, tiled=True)
 
 
+OWN, XG, DG = 0, 1, 2
+
+
+def kernel(
+    nf, npan, f_hbm, q_ref, bw_ref, out_ref,
+    own, scaled, xbuf, ubuf, dbuf, xs, ds, acc, keep, away, cxin, zout, zin, total, fwd, fin,
+    local_sem, fsend, frecv, csend, crecv, zsend, zrecv, gsend, grecv,
+):
+    rows, panels = own.shape
+    half = panels // 2
+    block = rows
+    freqs = rows // COMP
+    oct_rows = 8 * COMP
+    octs = rows // oct_rows
+    nz = npan // CORES
+    f32, bf16 = jnp.float32, jnp.bfloat16
+
+    f = lax.axis_index("freq")
+    p = lax.axis_index("panel")
+    z, core = p // CORES, lax.rem(p, CORES)
+    odd = lax.rem(f, 2)
+    mate = f + 1 - 2 * odd
+    has_u = f + 2 < nf
+    has_d = f >= 2
+    has_x = jnp.logical_or(odd == 1, has_u)
+    partner = p + 1 - 2 * core
+
+    def dev(ff, pp):
+        return {"freq": ff, "panel": pp}
+
+    load = pltpu.make_async_copy(f_hbm, own, local_sem)
+    load.start()
+
+    barrier = pltpu.get_barrier_semaphore()
+
+    def greet(ff, pp):
+        pl.semaphore_signal(barrier, inc=1, device_id=dev(ff, pp), device_id_type=MESH)
+
+    greet(mate, p)
+    greet(f, partner)
+    for zd in range(nz):
+        @pl.when(z != zd)
+        def _(zd=zd):
+            greet(f, zd * CORES + core)
+
+    @pl.when(has_u)
+    def _():
+        greet(f + 2, p)
+
+    @pl.when(has_d)
+    def _():
+        greet(f - 2, p)
+
+    count = 1 + nz + jnp.where(has_u, 1, 0) + jnp.where(has_d, 1, 0)
+    pl.semaphore_wait(barrier, count)
+
+    def half_at(which):
+        return pl.ds(pl.multiple_of(which * half, LANES), half)
+
+    def field_copy(which, dst, slot, ff):
+        return pltpu.make_async_remote_copy(
+            src_ref=f_hbm.at[:, half_at(which)], dst_ref=dst,
+            send_sem=fsend.at[slot], recv_sem=frecv.at[slot],
+            device_id=dev(ff, p), device_id_type=MESH,
+        )
+
+    to_mate = field_copy(1 - odd, xbuf, 0, mate)
+    to_lower = field_copy(0, ubuf, 1, f - 2)
+    to_upper = field_copy(1, dbuf, 2, f + 2)
+    to_mate.start()
+
+    @pl.when(has_d)
+    def _():
+        to_lower.start()
+
+    @pl.when(has_u)
+    def _():
+        to_upper.start()
+
+    def weight_at(where):
+        index = q_ref[:, where]
+        w = jnp.zeros(index.shape, f32)
+        for value, entry in enumerate(QUAD_TABLE):
+            w = jnp.where(index == value, jnp.float32(entry), w)
+        return w
+
+    def scale(src, dst, where):
+        w = weight_at(where)
+
+        def step(i, carry):
+            at = pl.ds(pl.multiple_of(i * 32, 32), 32)
+            dst[at, :] = (src[at, :].astype(f32) * w).astype(bf16)
+            return carry
+
+        lax.fori_loop(0, rows // 32, step, 0)
+
+    def gram(left, left_at, right, right_at, slot, rel):
+        tall = min(256, rows)
+
+        def step(i, carry):
+            at = pl.ds(pl.multiple_of(i * tall, tall), tall)
+            acc[slot, at, rel * block:(rel + 1) * block] = lax.dot_general(
+                left[at, left_at], right[:, right_at],
+                (((1,), (1,)), ((), ())), preferred_element_type=f32,
+            )
+            return carry
+
+        lax.fori_loop(0, rows // tall, step, 0)
+
+    def clear(slot, rel):
+        acc[slot, :, rel * block:(rel + 1) * block] = jnp.zeros((rows, block), f32)
+
+    clear(XG, 0)
+    clear(XG, 2)
+    clear(DG, 0)
+
+    @pl.when(odd == 0)
+    def _():
+        clear(DG, 1)
+
+    @pl.when(odd == 1)
+    def _():
+        clear(OWN, 1)
+
+    @pl.when(jnp.logical_not(has_u))
+    def _():
+        clear(OWN, 2)
+
+    load.wait()
+    everything = pl.ds(0, panels)
+    first = pl.ds(0, half)
+    second = pl.ds(half, half)
+    scale(own, scaled, everything)
+    gram(scaled, everything, own, everything, OWN, 0)
+
+    to_mate.wait_recv()
+    scale(xbuf, xs, half_at(odd))
+
+    @pl.when(odd == 0)
+    def _():
+        gram(scaled, first, xbuf, first, OWN, 1)
+
+    @pl.when(odd == 1)
+    def _():
+        gram(xs, first, own, second, XG, 1)
+
+    @pl.when(has_u)
+    def _():
+        to_lower.wait_recv()
+        gram(scaled, first, ubuf, first, OWN, 2)
+
+        @pl.when(odd == 0)
+        def _():
+            gram(xs, first, ubuf, first, XG, 1)
+
+    @pl.when(has_d)
+    def _():
+        to_upper.wait_recv()
+        scale(dbuf, ds, second)
+        gram(ds, first, own, second, DG, 2)
+
+        @pl.when(odd == 1)
+        def _():
+            gram(ds, first, xbuf, first, DG, 1)
+
+    def span(slot, zd):
+        lo_k, hi_k = zd * CORES, zd * CORES + CORES - 1
+        if slot == OWN:
+            return 0, octs
+        lo = max(0, octs - 1 - hi_k)
+        hi = min(octs - 1, 2 * octs - 1 - lo_k) if slot == XG else octs - 1
+        return lo, hi + 1
+
+    def tiles(slot, which, dst):
+        for zd in range(nz):
+            lo, hi = span(slot, zd)
+
+            def step(o, carry, zd=zd):
+                lane = pl.multiple_of((o + zd * CORES + which) * LANES, LANES)
+                for c in range(8):
+                    at = pl.ds(pl.multiple_of(o * oct_rows + c * COMP, COMP), COMP)
+                    if c == 7:
+                        lane_next = pl.multiple_of(lane + LANES, LANES)
+                        value = acc[slot, at, pl.ds(lane_next, LANES)]
+                    else:
+                        pair = acc[slot, at, pl.ds(lane, 2 * LANES)]
+                        value = pltpu.roll(pair, 2 * LANES - COMP * (c + 1), 1)[:, :LANES]
+                    dst[slot, zd, at, :] = value.astype(dst.dtype)
+                return carry
+
+            lax.fori_loop(lo, hi, step, 0)
+
+    def core_copy(slot, zd):
+        lo, hi = span(slot, zd)
+        at = pl.ds(lo * oct_rows, (hi - lo) * oct_rows)
+        return pltpu.make_async_remote_copy(
+            src_ref=away.at[slot, zd, at, :], dst_ref=cxin.at[slot, zd, at, :],
+            send_sem=csend.at[slot, zd], recv_sem=crecv.at[slot, zd],
+            device_id=dev(f, partner), device_id_type=MESH,
+        )
+
+    def z_copy(slot, zd, source):
+        lo, hi = span(slot, zd)
+        at = pl.ds(lo * oct_rows, (hi - lo) * oct_rows)
+        return pltpu.make_async_remote_copy(
+            src_ref=zout.at[slot, zd, at, :], dst_ref=zin.at[slot, source, at, :],
+            send_sem=zsend.at[slot, zd], recv_sem=zrecv.at[slot, source],
+            device_id=dev(f, zd * CORES + core), device_id_type=MESH,
+        )
+
+    def emit(slot):
+        tiles(slot, 1 - core, away)
+        for zd in range(nz):
+            core_copy(slot, zd).start()
+        tiles(slot, core, keep)
+
+    def relay(slot):
+        for zd in range(nz):
+            core_copy(slot, zd).wait_recv()
+            lo, hi = span(slot, zd)
+
+            def step(o, carry, zd=zd):
+                at = pl.ds(pl.multiple_of(o * oct_rows, oct_rows), oct_rows)
+                both = keep[slot, zd, at, :] + cxin[slot, zd, at, :].astype(f32)
+
+                @pl.when(z == zd)
+                def _():
+                    total[slot, at, :] = both
+
+                @pl.when(z != zd)
+                def _():
+                    zout[slot, zd, at, :] = both.astype(bf16)
+
+                return carry
+
+            lax.fori_loop(lo, hi, step, 0)
+
+            @pl.when(z != zd)
+            def _(zd=zd):
+                z_copy(slot, zd, z).start()
+
+    def gather(slot):
+        for zd in range(nz):
+            lo, hi = span(slot, zd)
+
+            @pl.when(z == zd)
+            def _(zd=zd, lo=lo, hi=hi):
+                for source in range(nz):
+                    if source == zd:
+                        continue
+                    z_copy(slot, zd, source).wait_recv()
+
+                def step(o, carry):
+                    at = pl.ds(pl.multiple_of(o * oct_rows, oct_rows), oct_rows)
+                    value = total[slot, at, :]
+                    for source in range(nz):
+                        if source != zd:
+                            value = value + zin[slot, source, at, :].astype(f32)
+                    total[slot, at, :] = value
+                    return carry
+
+                lax.fori_loop(lo, hi, step, 0)
+
+    def drain(slot):
+        for zd in range(nz):
+            core_copy(slot, zd).wait_send()
+
+            @pl.when(z != zd)
+            def _(zd=zd):
+                z_copy(slot, zd, z).wait_send()
+
+    def forward(slot, ff):
+        return pltpu.make_async_remote_copy(
+            src_ref=total.at[slot], dst_ref=fwd.at[slot],
+            send_sem=gsend.at[slot], recv_sem=grecv.at[slot],
+            device_id=dev(ff, p), device_id_type=MESH,
+        )
+
+    present = {OWN: None, XG: has_x, DG: has_d}
+
+    def each(order, act):
+        for slot in order:
+            if present[slot] is None:
+                act(slot)
+            else:
+                pl.when(present[slot])(functools.partial(act, slot))
+
+    total[XG] = jnp.zeros(total.shape[1:], f32)
+    total[DG] = jnp.zeros(total.shape[1:], f32)
+    order = (XG, DG, OWN)
+    each(order, emit)
+    each(order, relay)
+    give_x = forward(XG, mate)
+    give_d = forward(DG, f - 2)
+
+    @pl.when(has_x)
+    def _():
+        gather(XG)
+        give_x.start()
+
+    @pl.when(has_d)
+    def _():
+        gather(DG)
+        give_d.start()
+
+    gather(OWN)
+    mate_gives = jnp.logical_or(odd == 0, f + 1 < nf)
+
+    def take(slot):
+        def step(o, carry):
+            at = pl.ds(pl.multiple_of(o * oct_rows, oct_rows), oct_rows)
+            total[OWN, at, :] = total[OWN, at, :] + fwd[slot, at, :]
+            return carry
+
+        lax.fori_loop(0, octs, step, 0)
+
+    @pl.when(mate_gives)
+    def _():
+        give_x.wait_recv()
+        take(XG)
+
+    @pl.when(has_u)
+    def _():
+        give_d.wait_recv()
+        take(DG)
+
+    fin[...] = total[OWN]
+    eye = lax.broadcasted_iota(jnp.int32, (freqs, freqs), 0) == lax.broadcasted_iota(
+        jnp.int32, (freqs, freqs), 1
+    )
+    width = jnp.sum(
+        jnp.where(eye, jnp.broadcast_to(bw_ref[...].astype(f32), (freqs, freqs)), 0.0), 1, keepdims=True
+    )
+    width = jnp.broadcast_to(width, (freqs, LANES))
+    norm = jnp.float32(1.0 / math.sqrt(panels * npan))
+    part = lax.broadcasted_iota(jnp.int32, (freqs, LANES), 1) // COMP
+    for h in range(COMP // 8):
+        values = [fin[pl.ds(h * 8 + a, freqs, stride=COMP), :] for a in range(8)]
+        for bit in (1, 2, 4):
+            upper = lax.rem(part // bit, 2) == 1
+            fresh = list(values)
+            for i in range(8):
+                if i & bit:
+                    continue
+                j = i | bit
+                fresh[i] = jnp.where(upper, pltpu.roll(values[j], COMP * bit, 1), values[i])
+                fresh[j] = jnp.where(upper, values[j], pltpu.roll(values[i], LANES - COMP * bit, 1))
+            values = fresh
+        for k in range(8):
+            offset = (p * 8 + k + 1).astype(f32)
+            live = offset <= width
+            start = (k * (COMP // 8) + h) * LANES
+            out_ref[:, start:start + LANES] = jnp.where(live, values[k] * norm, 0.0)
+
+    to_mate.wait_send()
+
+    @pl.when(has_d)
+    def _():
+        to_lower.wait_send()
+        give_d.wait_send()
+
+    @pl.when(has_u)
+    def _():
+        to_upper.wait_send()
+
+    @pl.when(has_x)
+    def _():
+        give_x.wait_send()
+
+    each(order, drain)
+
+
+def fused(nf, npan, fields, quad_index, band_width):
+    freqs, comp, panels = fields.shape
+    rows = freqs * comp
+    nz = npan // CORES
+    half = panels // 2
+    out_cols = REACH * freqs * comp * comp // npan
+    bf16, f32 = jnp.bfloat16, jnp.float32
+    dma = pltpu.SemaphoreType.DMA
+    vmem = pl.BlockSpec(memory_space=pltpu.VMEM)
+    return pl.pallas_call(
+        functools.partial(kernel, nf, npan),
+        out_shape=jax.ShapeDtypeStruct((freqs, out_cols), f32),
+        in_specs=[pl.BlockSpec(memory_space=pl.ANY), vmem, vmem],
+        out_specs=vmem,
+        scratch_shapes=[
+            pltpu.VMEM((rows, panels), bf16),
+            pltpu.VMEM((rows, panels), bf16),
+            pltpu.VMEM((rows, half), bf16),
+            pltpu.VMEM((rows, half), bf16),
+            pltpu.VMEM((rows, half), bf16),
+            pltpu.VMEM((rows, half), bf16),
+            pltpu.VMEM((rows, half), bf16),
+            pltpu.VMEM((3, rows, (REACH + 1) * rows), f32),
+            pltpu.VMEM((3, nz, rows, LANES), f32),
+            pltpu.VMEM((3, nz, rows, LANES), bf16),
+            pltpu.VMEM((3, nz, rows, LANES), bf16),
+            pltpu.VMEM((3, nz, rows, LANES), bf16),
+            pltpu.VMEM((3, nz, rows, LANES), bf16),
+            pltpu.VMEM((3, rows, LANES), f32),
+            pltpu.VMEM((3, rows, LANES), f32),
+            pltpu.VMEM((rows, LANES), f32),
+            dma,
+            dma((3,)), dma((3,)),
+            dma((3, nz)), dma((3, nz)),
+            dma((3, nz)), dma((3, nz)),
+            dma((3,)), dma((3,)),
+        ],
+        compiler_params=pltpu.CompilerParams(
+            collective_id=0, has_side_effects=True, vmem_limit_bytes=58 * 1024 * 1024
+        ),
+    )(fields.reshape(rows, panels), quad_index.reshape(1, panels), band_width.reshape(1, freqs))
+
+
+def local(nf, npan, fields, quad_index, band_width):
+    freqs, comp, panels = fields.shape
+    share = REACH * freqs * comp // npan
+    fits = nf % 2 == 0 and npan % CORES == 0 and share == LANES and freqs % 8 == 0 and panels % (4 * LANES) == 0
+    if not fits:
+        return plain(fields, quad_index, band_width)
+    return fused(nf, npan, fields, quad_index, band_width)
+
+
 def solution(mesh):
     placed = (P("freq", None, "panel"), P("panel"), P("freq"))
     return jax.shard_map(
-        local, mesh=mesh, in_specs=placed, out_specs=P("freq", "panel"), check_vma=False
+        functools.partial(local, mesh.shape["freq"], mesh.shape["panel"]),
+        mesh=mesh, in_specs=placed, out_specs=P("freq", "panel"), check_vma=False,
     )

time: 287 us -> 75 us (0.26); the launches traced: 282 us -> 74.9 us
  waiting for transfers between devices: 173 us -> 0 us
  Pallas kernels: 0 us -> 73.2 us
  local copies, waits for them, and re-layouts: 72.4 us -> 1.67 us
  other arithmetic: 16.1 us -> 0 us
  between operations: 13.5 us -> 0.01 us
  starting transfers between devices: 3.86 us -> 0 us
  matrix products: 3.84 us -> 0 us
    reduce_scatter x1 -> x0, waiting for transfers between devices: 87.2 us -> none  [local(): return lax.psum_scatter(terms, 'panel', scatter_dimension=1, tiled=True)]
    ppermute x2 -> x0, waiting for transfers between devices: 85.4 us -> none  [shifted(): return lax.ppermute(x, axis, pairs)]
    pallas_call x0 -> x1, Pallas kernels: none -> 73.2 us  [fused(): pl.pallas_call(functools.partial(kernel, nf, npan), out_shape=jax.ShapeDt...]
    reshape x2 -> x0, local copies, waits for them, and re-layouts: 39.7 us -> none  [local(): jnp.concatenate(grams, 1)]
    gather x1 -> x0, local copies, waits for them, and re-layouts: 16.8 us -> none  [pick_band(): return lax.dynamic_slice_in_dim(block, row_index + 1, band, 1)]
    mul x1 -> x0, local copies, waits for them, and re-layouts: 13.6 us -> none  [local(): picked.reshape(freq_local, band * COMP * COMP)]
    mul x1 -> x0, other arithmetic: 12.2 us -> none  [local(): picked.reshape(freq_local, band * COMP * COMP)]
    ppermute x2 -> x0, starting transfers between devices: 3.86 us -> none  [shifted(): return lax.ppermute(x, axis, pairs)]
  transfers between devices with their start and end apart: 3 -> 0, of which waited for: 3 -> 0; matrix products, arithmetic and copies ran while one was open for 2% -> 0% of each run, Pallas kernels for 0% -> 0%
where the time goes in v1:
time: 75 us; the launch traced here: 74.9 us
  Pallas kernels  73.2 us (98%)
  local copies, waits for them, and re-layouts  1.67 us (2%)
    pallas_call x1, Pallas kernels, fused(): pl.pallas_call(functools.partial(kernel, nf, npan), out_shape=jax.ShapeDt...  73.2 us
    unnamed x1, local copies, waits for them, and re-layouts  1.67 us

profile of v1, /device:TPU:26, one launch (start us, length us, event | category | flops | bytes accessed | tf_op | source)
XLA Modules:
  0.0 74.9 jit_solution(14321766660427838623)
XLA Ops:
  0.0 73.2 %shard_map.37 = f32[32,2048]{1,0:T(8,128)} custom-call(bf16[512,2048]{1,0:T(8,128)(2,1)} %bitcast.3, s32[1,2048]{1,0:T(1,128)} %bitcast.4, s32[1,32]{1,0:T(1,128)} %bitcast.5), custom_call_target="tpu_custom_call" | custom-call | tf_op jit(solution)/shard_map/pallas_call | solution.py:446
  73.2 1.7 %copy.5 = f32[32,2048]{1,0:T(8,128)} copy(f32[32,2048]{1,0:T(8,128)} %shard_map.37) | data formatting | bytes 524288

commit v2 on v0

--- a/solution.py
+++ b/solution.py
@@ -1,13 +1,18 @@
+import functools
 import math
 
 import jax
 import jax.numpy as jnp
 from jax import lax
+from jax.experimental import pallas as pl
+from jax.experimental.pallas import tpu as pltpu
 from jax.sharding import PartitionSpec as P
 
 COMP = 16
 REACH = 2
-
+LANES = 128
+CORES = 2
+MESH = pl.DeviceIdType.MESH
 
 QUAD_TABLE = (0.2, 0.45, 0.8, 1.1, 1.6, 2.3)
 
@@ -18,7 +23,7 @@
     return lax.ppermute(x, axis, pairs)
 
 
-def local(fields, quad_index, band_width):
+def plain(fields, quad_index, band_width):
     freq_local = fields.shape[0]
     panel_local = fields.shape[2]
     band = REACH * freq_local
@@ -57,8 +62,493 @@
     return lax.psum_scatter(terms, "panel", scatter_dimension=1, tiled=True)
 
 
+OWN, XG, DG = 0, 1, 2
+
+
+def kernel(
+    nf, npan, f_hbm, q_ref, bw_ref, out_ref,
+    own, scaled, xbuf, ubuf, dbuf, xs, ds, acc, keep, away, cxin, zout, zin, total, fwd, fin,
+    local_sem, fsend, frecv, csend, crecv, zsend, zrecv, gsend, grecv,
+):
+    rows, panels = own.shape
+    half = panels // 2
+    block = rows
+    freqs = rows // COMP
+    oct_rows = 8 * COMP
+    octs = rows // oct_rows
+    nz = npan // CORES
+    f32, bf16 = jnp.float32, jnp.bfloat16
+
+    f = lax.axis_index("freq")
+    p = lax.axis_index("panel")
+    z, core = p // CORES, lax.rem(p, CORES)
+    odd = lax.rem(f, 2)
+    mate = f + 1 - 2 * odd
+    has_u = f + 2 < nf
+    has_d = f >= 2
+    has_x = jnp.logical_or(odd == 1, has_u)
+    partner = p + 1 - 2 * core
+
+    def dev(ff, pp):
+        return {"freq": ff, "panel": pp}
+
+    load = pltpu.make_async_copy(f_hbm, own, local_sem)
+    load.start()
+
+    barrier = pltpu.get_barrier_semaphore()
+
+    def greet(ff, pp):
+        pl.semaphore_signal(barrier, inc=1, device_id=dev(ff, pp), device_id_type=MESH)
+
+    greet(mate, p)
+    greet(f, partner)
+    for zd in range(nz):
+        @pl.when(z != zd)
+        def _(zd=zd):
+            greet(f, zd * CORES + core)
+
+    @pl.when(has_u)
+    def _():
+        greet(f + 2, p)
+
+    @pl.when(has_d)
+    def _():
+        greet(f - 2, p)
+
+    count = 1 + nz + jnp.where(has_u, 1, 0) + jnp.where(has_d, 1, 0)
+    pl.semaphore_wait(barrier, count)
+
+    def half_at(which):
+        return pl.ds(pl.multiple_of(which * half, LANES), half)
+
+    def rows_of(o, n=1):
+        return pl.ds(pl.multiple_of(o * oct_rows, oct_rows), n * oct_rows)
+
+    def field_copy(which, dst, slot, ff, o):
+        return pltpu.make_async_remote_copy(
+            src_ref=f_hbm.at[rows_of(o), half_at(which)], dst_ref=dst.at[rows_of(o), :],
+            send_sem=fsend.at[slot, o], recv_sem=frecv.at[slot, o],
+            device_id=dev(ff, p), device_id_type=MESH,
+        )
+
+    def to_mate(o):
+        return field_copy(1 - odd, xbuf, 0, mate, o)
+
+    def to_lower(o):
+        return field_copy(0, ubuf, 1, f - 2, o)
+
+    def to_upper(o):
+        return field_copy(1, dbuf, 2, f + 2, o)
+
+    for o in range(octs):
+        to_mate(o).start()
+
+        @pl.when(has_d)
+        def _(o=o):
+            to_lower(o).start()
+
+        @pl.when(has_u)
+        def _(o=o):
+            to_upper(o).start()
+
+    def weight_at(where):
+        index = q_ref[:, where]
+        w = jnp.zeros(index.shape, f32)
+        for value, entry in enumerate(QUAD_TABLE):
+            w = jnp.where(index == value, jnp.float32(entry), w)
+        return w
+
+    def scale(src, dst, where, o, n):
+        w = weight_at(where)
+
+        def step(i, carry):
+            at = pl.ds(pl.multiple_of(o * oct_rows + i * 32, 32), 32)
+            dst[at, :] = (src[at, :].astype(f32) * w).astype(bf16)
+            return carry
+
+        lax.fori_loop(0, n * oct_rows // 32, step, 0)
+
+    def gram(left, left_at, lo, n, right, right_at, ro, m, slot, rel):
+        tall = 2 if n % 2 == 0 else 1
+        first_col = rel * block + ro * oct_rows
+
+        def step(i, carry):
+            at = rows_of(lo + i * tall, tall)
+            acc[slot, at, first_col:first_col + m * oct_rows] = lax.dot_general(
+                left[at, left_at], right[ro * oct_rows:(ro + m) * oct_rows, right_at],
+                (((1,), (1,)), ((), ())), preferred_element_type=f32,
+            )
+            return carry
+
+        if n == tall:
+            step(0, 0)
+        else:
+            lax.fori_loop(0, n // tall, step, 0)
+
+    def clear(slot, tile):
+        acc[slot, :, tile * LANES:(tile + 1) * LANES] = jnp.zeros((rows, LANES), f32)
+
+    clear(XG, octs - 1)
+    clear(XG, 2 * octs)
+    clear(DG, octs - 1)
+
+    @pl.when(odd == 0)
+    def _():
+        clear(DG, 2 * octs - 1)
+
+    @pl.when(odd == 1)
+    def _():
+        clear(OWN, octs)
+        clear(OWN, 2 * octs - 1)
+
+    @pl.when(jnp.logical_not(has_u))
+    def _():
+        clear(OWN, 2 * octs)
+
+    def valid(slot, o, pp):
+        t = o + pp
+        low, high = t >= octs - 1, t <= 2 * octs - 1
+        if slot == OWN:
+            return jnp.logical_or(
+                t <= octs - 1,
+                jnp.logical_or(
+                    jnp.logical_and(odd == 0, high),
+                    jnp.logical_and(has_u, t >= 2 * octs - 1),
+                ),
+            )
+        if slot == XG:
+            return jnp.logical_and(has_x, jnp.logical_and(low, high))
+        upper = jnp.logical_or(t >= 2 * octs - 1, jnp.logical_and(odd == 1, low))
+        return jnp.logical_and(has_d, upper)
+
+    def core_copy(slot, o, pp):
+        zd = pp // CORES
+        return pltpu.make_async_remote_copy(
+            src_ref=away.at[slot, pp, rows_of(o), :], dst_ref=cxin.at[slot, zd, rows_of(o), :],
+            send_sem=csend.at[slot, zd, o], recv_sem=crecv.at[slot, zd, o],
+            device_id=dev(f, partner), device_id_type=MESH,
+        )
+
+    def z_copy(slot, o, zd, source):
+        return pltpu.make_async_remote_copy(
+            src_ref=zout.at[slot, zd, rows_of(o), :], dst_ref=zin.at[slot, source, rows_of(o), :],
+            send_sem=zsend.at[slot, zd, o], recv_sem=zrecv.at[slot, source, o],
+            device_id=dev(f, zd * CORES + core), device_id_type=MESH,
+        )
+
+    def walk(act, slot, o, t, n, do, dt):
+        def step(i, carry):
+            oo, tt = o + i * do, t + i * dt
+            act(slot, oo, tt - oo, tt)
+            return carry
+
+        if n > 0:
+            lax.fori_loop(0, n, step, 0)
+
+    def make(slot, o, pp, t):
+        lane = pl.multiple_of(t * LANES, LANES)
+        for c in range(8):
+            at = pl.ds(pl.multiple_of(o * oct_rows + c * COMP, COMP), COMP)
+            if c == 7:
+                value = acc[slot, at, pl.ds(pl.multiple_of(lane + LANES, LANES), LANES)]
+            else:
+                pair = acc[slot, at, pl.ds(lane, 2 * LANES)]
+                value = pltpu.roll(pair, 2 * LANES - COMP * (c + 1), 1)[:, :LANES]
+            keep[slot, pp, at, :] = value
+            away[slot, pp, at, :] = value.astype(bf16)
+
+        @pl.when(lax.rem(pp, CORES) != core)
+        def _():
+            core_copy(slot, o, pp).start()
+
+    def join(slot, o, pp, t):
+        @pl.when(lax.rem(pp, CORES) == core)
+        def _():
+            zd = pp // CORES
+            core_copy(slot, o, pp).wait_recv()
+            both = keep[slot, pp, rows_of(o), :] + cxin[slot, zd, rows_of(o), :].astype(f32)
+
+            @pl.when(z == zd)
+            def _():
+                total[slot, rows_of(o), :] = both
+
+            @pl.when(z != zd)
+            def _():
+                zout[slot, zd, rows_of(o), :] = both.astype(bf16)
+                z_copy(slot, o, zd, z).start()
+
+    def both_ways(jobs):
+        for act in (make, join):
+            for job in jobs:
+                if len(job) == 2:
+                    @pl.when(job[0])
+                    def _(job=job, act=act):
+                        for inner in job[1]:
+                            walk(act, *inner)
+                else:
+                    walk(act, *job)
+
+    load.wait()
+    everything = pl.ds(0, panels)
+    first = pl.ds(0, half)
+    second = pl.ds(half, half)
+    even_now, odd_now = odd == 0, odd == 1
+    scale(own, scaled, everything, 0, octs)
+    gram(scaled, everything, 0, octs, own, everything, 0, octs, OWN, 0)
+    jobs = [(OWN, 0, t, t + 1, 1, 0) for t in range(octs - 1)]
+    jobs.append((odd_now, [(OWN, 0, octs - 1, octs, 1, 0)]))
+    both_ways(jobs)
+
+    def corner(slot, i):
+        last = i == octs - 1
+        out = [(slot, i, octs - 1, i + 1 + last, 0, 1), (slot, 0, octs - 1 + i, i, 1, 0)]
+        if last:
+            out.append((slot, 0, 2 * octs - 1, i, 1, 0))
+        return out
+
+    for i in range(octs):
+        last = i == octs - 1
+        to_mate(i).wait_recv()
+        scale(xbuf, xs, half_at(odd), i, 1)
+        jobs = []
+
+        @pl.when(odd_now)
+        def _(i=i):
+            gram(xs, first, i, 1, own, second, 0, octs, XG, 1)
+
+        jobs.append((odd_now, [(XG, i, octs - 1, octs + 1, 0, 1)]))
+
+        @pl.when(even_now)
+        def _(i=i):
+            gram(scaled, first, 0, octs, xbuf, first, i, 1, OWN, 1)
+
+        @pl.when(has_u)
+        def _(i=i):
+            to_lower(i).wait_recv()
+            gram(scaled, first, i, octs - i, ubuf, first, i, 1, OWN, 2)
+
+        @pl.when(jnp.logical_and(has_u, even_now))
+        def _(i=i):
+            gram(xs, first, i, 1, ubuf, first, 0, i + 1, XG, 1)
+            if i:
+                gram(xs, first, 0, i, ubuf, first, i, 1, XG, 1)
+
+        jobs.append((jnp.logical_and(has_u, even_now), corner(XG, i)))
+
+        @pl.when(has_d)
+        def _(i=i):
+            to_upper(i).wait_recv()
+            scale(dbuf, ds, second, i, 1)
+            gram(ds, first, i, 1, own, second, 0, i + 1, DG, 2)
+
+        @pl.when(jnp.logical_and(has_d, odd_now))
+        def _(i=i):
+            gram(ds, first, i, 1, xbuf, first, 0, i + 1, DG, 1)
+            if i:
+                gram(ds, first, 0, i, xbuf, first, i, 1, DG, 1)
+
+        jobs.append((jnp.logical_and(has_d, odd_now), corner(DG, i) + [(DG, i, 2 * octs, i, 0, 1)]))
+        jobs.append((jnp.logical_and(has_d, even_now), [(DG, i, 2 * octs - 1, i + 1, 0, 1)]))
+        own_even = [(OWN, 0, octs - 1 + i, octs, 1, 0)]
+        if last:
+            own_even.append((OWN, 0, 2 * octs - 1, octs, 1, 0))
+        jobs.append((even_now, own_even))
+        if i == 0:
+            jobs.append((jnp.logical_and(has_u, odd_now), [(OWN, 0, 2 * octs - 1, octs, 1, 0)]))
+        else:
+            jobs.append((has_u, [(OWN, i, 2 * octs - 1 + i, octs - i, 1, 0)]))
+        both_ways(jobs)
+
+    def forward(slot, ff, o):
+        return pltpu.make_async_remote_copy(
+            src_ref=total.at[slot, rows_of(o), :], dst_ref=fwd.at[slot, rows_of(o), :],
+            send_sem=gsend.at[slot, o], recv_sem=grecv.at[slot, o],
+            device_id=dev(ff, p), device_id_type=MESH,
+        )
+
+    def settle(slot, target):
+        def step(o, carry):
+            here = valid(slot, o, p)
+
+            @pl.when(here)
+            def _():
+                value = total[slot, rows_of(o), :]
+                for hop in range(1, nz):
+                    source = lax.rem(z + hop, nz)
+                    z_copy(slot, o, z, source).wait_recv()
+                    value = value + zin[slot, source, rows_of(o), :].astype(f32)
+                total[slot, rows_of(o), :] = value
+                if target is not None:
+                    forward(slot, target, o).start()
+
+            if target is None:
+                @pl.when(jnp.logical_not(here))
+                def _():
+                    total[slot, rows_of(o), :] = jnp.zeros((oct_rows, LANES), f32)
+
+            return carry
+
+        lax.fori_loop(0, octs, step, 0)
+
+    settle(XG, mate)
+    settle(DG, f - 2)
+    settle(OWN, None)
+
+    def drain(slot):
+        def step(i, carry):
+            pp, o = i // octs, lax.rem(i, octs)
+            zd = pp // CORES
+
+            @pl.when(valid(slot, o, pp))
+            def _():
+                @pl.when(lax.rem(pp, CORES) != core)
+                def _():
+                    core_copy(slot, o, pp).wait_send()
+
+                @pl.when(jnp.logical_and(lax.rem(pp, CORES) == core, z != zd))
+                def _():
+                    z_copy(slot, o, zd, z).wait_send()
+
+            return carry
+
+        lax.fori_loop(0, npan * octs, step, 0)
+
+    for slot in (OWN, XG, DG):
+        drain(slot)
+
+    mate_gives = jnp.logical_or(odd == 0, f + 1 < nf)
+
+    def take(slot, giver, comes):
+        def step(o, carry):
+            @pl.when(comes(o))
+            def _():
+                forward(slot, giver, o).wait_recv()
+                total[OWN, rows_of(o), :] = total[OWN, rows_of(o), :] + fwd[slot, rows_of(o), :]
+
+            return carry
+
+        lax.fori_loop(0, octs, step, 0)
+
+    def from_mate(o):
+        t = o + p
+        return jnp.logical_and(mate_gives, jnp.logical_and(t >= octs - 1, t <= 2 * octs - 1))
+
+    def from_upper(o):
+        t = o + p
+        reach = jnp.logical_or(t >= 2 * octs - 1, jnp.logical_and(odd == 1, t >= octs - 1))
+        return jnp.logical_and(has_u, reach)
+
+    take(XG, mate, from_mate)
+    take(DG, f - 2, from_upper)
+
+    fin[...] = total[OWN]
+    eye = lax.broadcasted_iota(jnp.int32, (freqs, freqs), 0) == lax.broadcasted_iota(
+        jnp.int32, (freqs, freqs), 1
+    )
+    width = jnp.sum(
+        jnp.where(eye, jnp.broadcast_to(bw_ref[...].astype(f32), (freqs, freqs)), 0.0), 1, keepdims=True
+    )
+    width = jnp.broadcast_to(width, (freqs, LANES))
+    norm = jnp.float32(1.0 / math.sqrt(panels * npan))
+    part = lax.broadcasted_iota(jnp.int32, (freqs, LANES), 1) // COMP
+    for h in range(COMP // 8):
+        values = [fin[pl.ds(h * 8 + a, freqs, stride=COMP), :] for a in range(8)]
+        for bit in (1, 2, 4):
+            upper = lax.rem(part // bit, 2) == 1
+            fresh = list(values)
+            for i in range(8):
+                if i & bit:
+                    continue
+                j = i | bit
+                fresh[i] = jnp.where(upper, pltpu.roll(values[j], COMP * bit, 1), values[i])
+                fresh[j] = jnp.where(upper, values[j], pltpu.roll(values[i], LANES - COMP * bit, 1))
+            values = fresh
+        for k in range(8):
+            offset = (p * 8 + k + 1).astype(f32)
+            live = offset <= width
+            start = (k * (COMP // 8) + h) * LANES
+            out_ref[:, start:start + LANES] = jnp.where(live, values[k] * norm, 0.0)
+
+    def close(o, carry):
+        to_mate(o).wait_send()
+
+        @pl.when(has_d)
+        def _():
+            to_lower(o).wait_send()
+
+        @pl.when(has_u)
+        def _():
+            to_upper(o).wait_send()
+
+        @pl.when(valid(XG, o, p))
+        def _():
+            forward(XG, mate, o).wait_send()
+
+        @pl.when(valid(DG, o, p))
+        def _():
+            forward(DG, f - 2, o).wait_send()
+
+        return carry
+
+    lax.fori_loop(0, octs, close, 0)
+
+
+def fused(nf, npan, fields, quad_index, band_width):
+    freqs, comp, panels = fields.shape
+    rows = freqs * comp
+    nz = npan // CORES
+    half = panels // 2
+    octs = freqs // 8
+    out_cols = REACH * freqs * comp * comp // npan
+    bf16, f32 = jnp.bfloat16, jnp.float32
+    dma = pltpu.SemaphoreType.DMA
+    vmem = pl.BlockSpec(memory_space=pltpu.VMEM)
+    return pl.pallas_call(
+        functools.partial(kernel, nf, npan),
+        out_shape=jax.ShapeDtypeStruct((freqs, out_cols), f32),
+        in_specs=[pl.BlockSpec(memory_space=pl.ANY), vmem, vmem],
+        out_specs=vmem,
+        scratch_shapes=[
+            pltpu.VMEM((rows, panels), bf16),
+            pltpu.VMEM((rows, panels), bf16),
+            pltpu.VMEM((rows, half), bf16),
+            pltpu.VMEM((rows, half), bf16),
+            pltpu.VMEM((rows, half), bf16),
+            pltpu.VMEM((rows, half), bf16),
+            pltpu.VMEM((rows, half), bf16),
+            pltpu.VMEM((3, rows, (REACH + 1) * rows), f32),
+            pltpu.VMEM((3, npan, rows, LANES), f32),
+            pltpu.VMEM((3, npan, rows, LANES), bf16),
+            pltpu.VMEM((3, nz, rows, LANES), bf16),
+            pltpu.VMEM((3, nz, rows, LANES), bf16),
+            pltpu.VMEM((3, nz, rows, LANES), bf16),
+            pltpu.VMEM((3, rows, LANES), f32),
+            pltpu.VMEM((3, rows, LANES), f32),
+            pltpu.VMEM((rows, LANES), f32),
+            dma,
+            dma((3, octs)), dma((3, octs)),
+            dma((3, nz, octs)), dma((3, nz, octs)),
+            dma((3, nz, octs)), dma((3, nz, octs)),
+            dma((3, octs)), dma((3, octs)),
+        ],
+        compiler_params=pltpu.CompilerParams(
+            collective_id=0, has_side_effects=True, vmem_limit_bytes=58 * 1024 * 1024
+        ),
+    )(fields.reshape(rows, panels), quad_index.reshape(1, panels), band_width.reshape(1, freqs))
+
+
+def local(nf, npan, fields, quad_index, band_width):
+    freqs, comp, panels = fields.shape
+    share = REACH * freqs * comp // npan
+    fits = nf % 2 == 0 and npan % CORES == 0 and share == LANES and freqs % 8 == 0 and panels % (4 * LANES) == 0
+    if not fits:
+        return plain(fields, quad_index, band_width)
+    return fused(nf, npan, fields, quad_index, band_width)
+
+
 def solution(mesh):
     placed = (P("freq", None, "panel"), P("panel"), P("freq"))
     return jax.shard_map(
-        local, mesh=mesh, in_specs=placed, out_specs=P("freq", "panel"), check_vma=False
+        functools.partial(local, mesh.shape["freq"], mesh.shape["panel"]),
+        mesh=mesh, in_specs=placed, out_specs=P("freq", "panel"), check_vma=False,
     )

time: 287 us -> 51.7 us (0.18); the launches traced: 282 us -> 50.7 us
  waiting for transfers between devices: 173 us -> 0 us
  local copies, waits for them, and re-layouts: 72.4 us -> 1.67 us
  Pallas kernels: 0 us -> 49 us
  other arithmetic: 16.1 us -> 0 us
  between operations: 13.5 us -> 0.01 us
  starting transfers between devices: 3.86 us -> 0 us
  matrix products: 3.84 us -> 0 us
    reduce_scatter x1 -> x0, waiting for transfers between devices: 87.2 us -> none  [local(): return lax.psum_scatter(terms, 'panel', scatter_dimension=1, tiled=True)]
    ppermute x2 -> x0, waiting for transfers between devices: 85.4 us -> none  [shifted(): return lax.ppermute(x, axis, pairs)]
    pallas_call x0 -> x1, Pallas kernels: none -> 49 us  [fused(): pl.pallas_call(functools.partial(kernel, nf, npan), out_shape=jax.ShapeDt...]
    reshape x2 -> x0, local copies, waits for them, and re-layouts: 39.7 us -> none  [local(): jnp.concatenate(grams, 1)]
    gather x1 -> x0, local copies, waits for them, and re-layouts: 16.8 us -> none  [pick_band(): return lax.dynamic_slice_in_dim(block, row_index + 1, band, 1)]
    mul x1 -> x0, local copies, waits for them, and re-layouts: 13.6 us -> none  [local(): picked.reshape(freq_local, band * COMP * COMP)]
    mul x1 -> x0, other arithmetic: 12.2 us -> none  [local(): picked.reshape(freq_local, band * COMP * COMP)]
    ppermute x2 -> x0, starting transfers between devices: 3.86 us -> none  [shifted(): return lax.ppermute(x, axis, pairs)]
  transfers between devices with their start and end apart: 3 -> 0, of which waited for: 3 -> 0; matrix products, arithmetic and copies ran while one was open for 2% -> 0% of each run, Pallas kernels for 0% -> 0%
where the time goes in v2:
time: 51.7 us; the launch traced here: 50.7 us
  Pallas kernels  49 us (95%)
  local copies, waits for them, and re-layouts  1.67 us (3%)
    pallas_call x1, Pallas kernels, fused(): pl.pallas_call(functools.partial(kernel, nf, npan), out_shape=jax.ShapeDt...  49 us
    unnamed x1, local copies, waits for them, and re-layouts  1.67 us

profile of v2, /device:TPU:26, one launch (start us, length us, event | category | flops | bytes accessed | tf_op | source)
XLA Modules:
  0.0 50.7 jit_solution(10346288271387438356)
XLA Ops:
  0.0 49.0 %shard_map.37 = f32[32,2048]{1,0:T(8,128)} custom-call(bf16[512,2048]{1,0:T(8,128)(2,1)} %bitcast.3, s32[1,2048]{1,0:T(1,128)} %bitcast.4, s32[1,32]{1,0:T(1,128)} %bitcast.5), custom_call_target="tpu_custom_call" | custom-call | tf_op jit(solution)/shard_map/pallas_call | solution.py:506
  49.0 1.7 %copy.5 = f32[32,2048]{1,0:T(8,128)} copy(f32[32,2048]{1,0:T(8,128)} %shard_map.37) | data formatting | bytes 524288

commit v3 on v2

--- a/solution.py
+++ b/solution.py
@@ -141,7 +141,7 @@
         return field_copy(1, dbuf, 2, f + 2, o)
 
     for o in range(octs):
-        to_mate(o).start()
+        to_mate(octs - 1 - o).start()
 
         @pl.when(has_d)
         def _(o=o):
@@ -149,7 +149,7 @@
 
         @pl.when(has_u)
         def _(o=o):
-            to_upper(o).start()
+            to_upper(octs - 1 - o).start()
 
     def weight_at(where):
         index = q_ref[:, where]
@@ -299,28 +299,22 @@
     jobs.append((odd_now, [(OWN, 0, octs - 1, octs, 1, 0)]))
     both_ways(jobs)
 
-    def corner(slot, i):
+    for i in range(octs):
+        x = octs - 1 - i
         last = i == octs - 1
-        out = [(slot, i, octs - 1, i + 1 + last, 0, 1), (slot, 0, octs - 1 + i, i, 1, 0)]
-        if last:
-            out.append((slot, 0, 2 * octs - 1, i, 1, 0))
-        return out
-
-    for i in range(octs):
-        last = i == octs - 1
-        to_mate(i).wait_recv()
-        scale(xbuf, xs, half_at(odd), i, 1)
+        to_mate(x).wait_recv()
+        scale(xbuf, xs, half_at(odd), x, 1)
         jobs = []
 
         @pl.when(odd_now)
-        def _(i=i):
-            gram(xs, first, i, 1, own, second, 0, octs, XG, 1)
-
-        jobs.append((odd_now, [(XG, i, octs - 1, octs + 1, 0, 1)]))
+        def _(x=x):
+            gram(xs, first, x, 1, own, second, 0, octs, XG, 1)
+
+        jobs.append((odd_now, [(XG, x, octs - 1, octs + 1, 0, 1)]))
 
         @pl.when(even_now)
-        def _(i=i):
-            gram(scaled, first, 0, octs, xbuf, first, i, 1, OWN, 1)
+        def _(x=x):
+            gram(scaled, first, 0, octs, xbuf, first, x, 1, OWN, 1)
 
         @pl.when(has_u)
         def _(i=i):
@@ -328,30 +322,40 @@
             gram(scaled, first, i, octs - i, ubuf, first, i, 1, OWN, 2)
 
         @pl.when(jnp.logical_and(has_u, even_now))
-        def _(i=i):
-            gram(xs, first, i, 1, ubuf, first, 0, i + 1, XG, 1)
+        def _(i=i, x=x):
+            gram(xs, first, x, 1, ubuf, first, 0, i + 1, XG, 1)
             if i:
-                gram(xs, first, 0, i, ubuf, first, i, 1, XG, 1)
-
-        jobs.append((jnp.logical_and(has_u, even_now), corner(XG, i)))
+                gram(xs, first, x + 1, i, ubuf, first, i, 1, XG, 1)
+
+        mixed = [(XG, x, octs - 1, i + 1 + last, 0, 1), (XG, x + 1, octs - 1 + i, i, 1, 0)]
+        if last:
+            mixed.append((XG, x + 1, 2 * octs - 1, i, 1, 0))
+        jobs.append((jnp.logical_and(has_u, even_now), mixed))
 
         @pl.when(has_d)
-        def _(i=i):
-            to_upper(i).wait_recv()
-            scale(dbuf, ds, second, i, 1)
-            gram(ds, first, i, 1, own, second, 0, i + 1, DG, 2)
+        def _(x=x):
+            to_upper(x).wait_recv()
+            scale(dbuf, ds, second, x, 1)
+            gram(ds, first, x, 1, own, second, 0, x + 1, DG, 2)
 
         @pl.when(jnp.logical_and(has_d, odd_now))
-        def _(i=i):
-            gram(ds, first, i, 1, xbuf, first, 0, i + 1, DG, 1)
+        def _(i=i, x=x):
+            gram(ds, first, x, 1, xbuf, first, x, i + 1, DG, 1)
             if i:
-                gram(ds, first, 0, i, xbuf, first, i, 1, DG, 1)
-
-        jobs.append((jnp.logical_and(has_d, odd_now), corner(DG, i) + [(DG, i, 2 * octs, i, 0, 1)]))
-        jobs.append((jnp.logical_and(has_d, even_now), [(DG, i, 2 * octs - 1, i + 1, 0, 1)]))
-        own_even = [(OWN, 0, octs - 1 + i, octs, 1, 0)]
+                gram(ds, first, x + 1, i, xbuf, first, x, 1, DG, 1)
+
+        mixed = [
+            (DG, x, octs + x - last, i + 1 + last, 0, 1),
+            (DG, x + 1, octs + x, i, 1, 0),
+            (DG, x, 2 * octs, x, 0, 1),
+        ]
         if last:
-            own_even.append((OWN, 0, 2 * octs - 1, octs, 1, 0))
+            mixed.append((DG, x + 1, octs - 1, i, 1, 0))
+        jobs.append((jnp.logical_and(has_d, odd_now), mixed))
+        jobs.append((jnp.logical_and(has_d, even_now), [(DG, x, 2 * octs - 1, x + 1, 0, 1)]))
+        own_even = [(OWN, 0, octs + x, octs, 1, 0)]
+        if last:
+            own_even.append((OWN, 0, octs - 1, octs, 1, 0))
         jobs.append((even_now, own_even))
         if i == 0:
             jobs.append((jnp.logical_and(has_u, odd_now), [(OWN, 0, 2 * octs - 1, octs, 1, 0)]))

time: 51.7 us -> 49.8 us (0.963); the launches traced: 50.7 us -> 49.6 us
  Pallas kernels: 49 us -> 47.9 us
    pallas_call x1, Pallas kernels: 49 us -> 47.9 us  [fused(): pl.pallas_call(functools.partial(kernel, nf, npan), out_shape=jax.ShapeDt...]
where the time goes in v3:
time: 49.8 us; the launch traced here: 49.6 us
  Pallas kernels  47.9 us (96%)
  local copies, waits for them, and re-layouts  1.67 us (3%)
    pallas_call x1, Pallas kernels, fused(): pl.pallas_call(functools.partial(kernel, nf, npan), out_shape=jax.ShapeDt...  47.9 us
    unnamed x1, local copies, waits for them, and re-layouts  1.67 us

profile of v3, /device:TPU:26, one launch (start us, length us, event | category | flops | bytes accessed | tf_op | source)
XLA Modules:
  0.0 49.6 jit_solution(15535610312714351409)
XLA Ops:
  0.0 47.9 %shard_map.37 = f32[32,2048]{1,0:T(8,128)} custom-call(bf16[512,2048]{1,0:T(8,128)(2,1)} %bitcast.3, s32[1,2048]{1,0:T(1,128)} %bitcast.4, s32[1,32]{1,0:T(1,128)} %bitcast.5), custom_call_target="tpu_custom_call" | custom-call | tf_op jit(solution)/shard_map/pallas_call | solution.py:510
  47.9 1.7 %copy.5 = f32[32,2048]{1,0:T(8,128)} copy(f32[32,2048]{1,0:T(8,128)} %shard_map.37) | data formatting | bytes 524288

commit v4 on v3

--- a/solution.py
+++ b/solution.py
@@ -278,15 +278,30 @@
                 z_copy(slot, o, zd, z).start()
 
     def both_ways(jobs):
-        for act in (make, join):
-            for job in jobs:
-                if len(job) == 2:
-                    @pl.when(job[0])
-                    def _(job=job, act=act):
-                        for inner in job[1]:
-                            walk(act, *inner)
-                else:
-                    walk(act, *job)
+        flat = []
+        for job in jobs:
+            if len(job) == 2:
+                flat.extend((job[0], inner) for inner in job[1] if inner[3] > 0)
+            else:
+                flat.append((None, job))
+
+        def run(act, entry):
+            when, inner = entry
+            if when is None:
+                walk(act, *inner)
+            else:
+                pl.when(when)(functools.partial(walk, act, *inner))
+
+        previous = {}
+        for entry in flat:
+            role = id(entry[0])
+            run(make, entry)
+            if role in previous:
+                run(join, previous[role])
+            previous[role] = entry
+        for entry in flat:
+            if previous[id(entry[0])] is entry:
+                run(join, entry)
 
     load.wait()
     everything = pl.ds(0, panels)

time: 49.8 us -> 51.2 us (1.028)
  Pallas kernels: 47.9 us -> 49.3 us
    pallas_call x1, Pallas kernels: 47.9 us -> 49.3 us  [fused(): pl.pallas_call(functools.partial(kernel, nf, npan), out_shape=jax.ShapeDt...]
where the time goes in v4:
time: 51.2 us; the launch traced here: 51 us
  Pallas kernels  49.3 us (96%)
  local copies, waits for them, and re-layouts  1.67 us (3%)
    pallas_call x1, Pallas kernels, fused(): pl.pallas_call(functools.partial(kernel, nf, npan), out_shape=jax.ShapeDt...  49.3 us
    unnamed x1, local copies, waits for them, and re-layouts  1.67 us

profile of v4, /device:TPU:26, one launch (start us, length us, event | category | flops | bytes accessed | tf_op | source)
XLA Modules:
  0.0 51.0 jit_solution(18268875346913117955)
XLA Ops:
  0.0 49.3 %shard_map.37 = f32[32,2048]{1,0:T(8,128)} custom-call(bf16[512,2048]{1,0:T(8,128)(2,1)} %bitcast.3, s32[1,2048]{1,0:T(1,128)} %bitcast.4, s32[1,32]{1,0:T(1,128)} %bitcast.5), custom_call_target="tpu_custom_call" | custom-call | tf_op jit(solution)/shard_map/pallas_call | solution.py:525
  49.3 1.7 %copy.5 = f32[32,2048]{1,0:T(8,128)} copy(f32[32,2048]{1,0:T(8,128)} %shard_map.37) | data formatting | bytes 524288

commit v5 on v3

--- a/solution.py
+++ b/solution.py
@@ -67,7 +67,7 @@
 
 def kernel(
     nf, npan, f_hbm, q_ref, bw_ref, out_ref,
-    own, scaled, xbuf, ubuf, dbuf, xs, ds, acc, keep, away, cxin, zout, zin, total, fwd, fin,
+    own, scaled, xbuf, ubuf, dbuf, xs, ds, acc, keep, away, cxin, zout, zin, total, give, fwd, fin,
     local_sem, fsend, frecv, csend, crecv, zsend, zrecv, gsend, grecv,
 ):
     rows, panels = own.shape
@@ -365,7 +365,7 @@
 
     def forward(slot, ff, o):
         return pltpu.make_async_remote_copy(
-            src_ref=total.at[slot, rows_of(o), :], dst_ref=fwd.at[slot, rows_of(o), :],
+            src_ref=give.at[slot, rows_of(o), :], dst_ref=fwd.at[slot, rows_of(o), :],
             send_sem=gsend.at[slot, o], recv_sem=grecv.at[slot, o],
             device_id=dev(ff, p), device_id_type=MESH,
         )
@@ -383,6 +383,7 @@
                     value = value + zin[slot, source, rows_of(o), :].astype(f32)
                 total[slot, rows_of(o), :] = value
                 if target is not None:
+                    give[slot, rows_of(o), :] = value.astype(bf16)
                     forward(slot, target, o).start()
 
             if target is None:
@@ -427,7 +428,7 @@
             @pl.when(comes(o))
             def _():
                 forward(slot, giver, o).wait_recv()
-                total[OWN, rows_of(o), :] = total[OWN, rows_of(o), :] + fwd[slot, rows_of(o), :]
+                total[OWN, rows_of(o), :] = total[OWN, rows_of(o), :] + fwd[slot, rows_of(o), :].astype(f32)
 
             return carry
 
@@ -527,7 +528,8 @@
             pltpu.VMEM((3, nz, rows, LANES), bf16),
             pltpu.VMEM((3, nz, rows, LANES), bf16),
             pltpu.VMEM((3, rows, LANES), f32),
-            pltpu.VMEM((3, rows, LANES), f32),
+            pltpu.VMEM((3, rows, LANES), bf16),
+            pltpu.VMEM((3, rows, LANES), bf16),
             pltpu.VMEM((rows, LANES), f32),
             dma,
             dma((3, octs)), dma((3, octs)),

time: 49.8 us -> 49.7 us (level)
  the two profiles are of different devices: /device:TPU:26 before, /device:TPU:0 now
where the time goes in v5:
time: 49.7 us; the launch traced here: 49.5 us
  Pallas kernels  47.8 us (96%)
  local copies, waits for them, and re-layouts  1.67 us (3%)
    pallas_call x1, Pallas kernels, fused(): pl.pallas_call(functools.partial(kernel, nf, npan), out_shape=jax.ShapeDt...  47.8 us
    unnamed x1, local copies, waits for them, and re-layouts  1.67 us

profile of v5, /device:TPU:0, one launch (start us, length us, event | category | flops | bytes accessed | tf_op | source)
XLA Modules:
  0.0 49.5 jit_solution(7391131065126980879)
XLA Ops:
  0.0 47.8 %shard_map.37 = f32[32,2048]{1,0:T(8,128)} custom-call(bf16[512,2048]{1,0:T(8,128)(2,1)} %bitcast.3, s32[1,2048]{1,0:T(1,128)} %bitcast.4, s32[1,32]{1,0:T(1,128)} %bitcast.5), custom_call_target="tpu_custom_call" | custom-call | tf_op jit(solution)/shard_map/pallas_call | solution.py:511
  47.8 1.7 %copy.5 = f32[32,2048]{1,0:T(8,128)} copy(f32[32,2048]{1,0:T(8,128)} %shard_map.37) | data formatting | bytes 524288
